TPU v7x, 256 devices: a whole 4x4x8 slice. The times are simulated.
256 devices in a mesh: member: 64 (over z_lo, x, y, core), shard: 4 (over z_hi).
Axes of the slice: x: 4, y: 4, z: 8 (z_hi: 4, z_lo: 2; z = z_hi * 2 + z_lo), core: 2. Of those that a mesh axis runs over, the one named last changes fastest.
Arguments:
- processor_latent: bfloat16 [64, 128, 1024], P('member', 'shard'), may hold values from -240 to 240
- stencil_index: int32 [4, 3, 768], P('shard'), may hold values from 0 to 127
- interp_weight: float32 [4, 3, 768], P('shard'), may hold values from 0.1 to 1
- prev_state: float32 [4, 112, 768], P('shard'), may hold values from -6 to 6
- observed: float32 [4, 112, 768], P('shard', None, 'member'), may hold values from -6 to 6
- cell_area: float32 [4, 768], P('shard', 'member'), may hold values from 0.5 to 2
- var_weight: float32 [112], replicated, may hold values from 1 to 16
- hidden_weight: bfloat16 [1024, 1024], replicated, may hold values from -0.1875 to 0.1875
- hidden_bias: float32 [1024], replicated, may hold values from -3 to 3
- output_weight: bfloat16 [1024, 112], replicated, may hold values from -0.1875 to 0.1875
- output_bias: float32 [112], replicated, may hold values from -3 to 3
Outputs:
- mesh_grad: float32 [64, 128, 1024], P('member', 'shard')
Inputs may be any that keep to these rules, and one draw needn't show every extreme that they name: `stencil_index`: rows of the same member's mesh.
All inputs are finite; a program needn't handle non-finite values.
Results may differ from a plain program's by a relative error of at most 0.019.
Values may be sent and summed in bfloat16 or wider, within the bound.
A program may use at most 64 MiB of HBM per device.

v0:
```python
import jax
import jax.numpy as jnp
from jax import lax
from jax.sharding import PartitionSpec as P

smoothing = 0.05
fairness = 0.95
epsilon = 1e-05


def softened_slope(differ):
    return differ / jnp.sqrt(differ * differ + smoothing * smoothing)


def normalize(latent):
    average = jnp.mean(latent, axis=1, keepdims=True)
    centred = latent - average
    inverse = lax.rsqrt(jnp.mean(centred * centred, axis=1, keepdims=True) + epsilon)
    return (centred * inverse, inverse)


def stencil_matrix(stencil, weights, row_count):
    row_ids = lax.iota(jnp.int32, row_count)
    hits = stencil[:, :, None] == row_ids[None, None, :]
    return jnp.sum(jnp.where(hits, weights[:, :, None], 0.0), axis=0)


def decode_members(normed, hidden_weight, hidden_bias, output_weight, output_bias, previous):
    pre_act = jnp.dot(normed, hidden_weight, preferred_element_type=jnp.float32) + hidden_bias
    hidden = jax.nn.silu(pre_act).astype(jnp.bfloat16)
    update = lax.dot_general(
        output_weight, hidden, (((0,), (1,)), ((), ())), preferred_element_type=jnp.float32
    )
    return (previous + (update + output_bias[:, None]), pre_act)


def local(
    processor_latent,
    stencil_index,
    interp_weight,
    prev_state,
    observed,
    cell_area,
    var_weight,
    hidden_weight,
    hidden_bias,
    output_weight,
    output_bias,
):
    mesh_local = processor_latent[0]
    stencil = stencil_index[0]
    weights = interp_weight[0]
    previous = prev_state[0]
    cell_count = stencil.shape[1]
    features = mesh_local.shape[1]
    variables = previous.shape[0]
    members = lax.axis_size("member")
    block_cells = cell_count // members
    shard_rows = lax.all_gather(mesh_local, "shard", axis=0, tiled=True)
    matrix = stencil_matrix(stencil, weights, shard_rows.shape[0])
    latent = jnp.dot(
        matrix,
        shard_rows.astype(jnp.float32),
        precision=lax.Precision.HIGHEST,
        preferred_element_type=jnp.float32,
    )
    normal_form, inverse = normalize(latent)
    normed = normal_form.astype(jnp.bfloat16)
    fairness_factor = (1.0 - fairness) / members
    bounds = (0, block_cells)
    arranged = normed.reshape(members, block_cells, features)
    earlier = previous.reshape(variables, members, block_cells)
    first_cell, stop_cell = bounds
    width_part = stop_cell - first_cell
    piece_rows = arranged.reshape(-1, features)
    prior_piece = earlier.reshape(variables, -1)
    prediction_piece, preactivation_piece = decode_members(
        piece_rows, hidden_weight, hidden_bias, output_weight, output_bias, prior_piece
    )
    received = lax.all_to_all(
        prediction_piece[None], "member", split_axis=2, concat_axis=0, tiled=True
    )
    stored = preactivation_piece.reshape(members, width_part, -1)
    pre_act = stored.reshape(cell_count, -1)
    flattened = received.reshape(members, -1)
    groups = flattened.reshape(members // 8, 8, -1)

    def group_pairs(chosen):
        return jnp.sum(softened_slope(chosen[:, None] - flattened[None]), axis=1)

    pairwise_sums = lax.map(group_pairs, groups).reshape(received.shape)
    loss_weighting = cell_area[0][None, None, :] * var_weight[None, :, None]
    slopes = (
        loss_weighting
        * (
            softened_slope(received - observed[0][None])
            - (1.0 - fairness_factor) / (members - 1) * pairwise_sums
        )
    ).astype(jnp.bfloat16)
    upstream_gradient = lax.all_to_all(slopes, "member", split_axis=0, concat_axis=2, tiled=True)[0]
    grad_hidden = lax.dot_general(
        upstream_gradient,
        output_weight,
        (((0,), (1,)), ((), ())),
        preferred_element_type=jnp.float32,
    )
    logistic = jax.nn.sigmoid(pre_act)
    grad_pre = (grad_hidden * (logistic * (1.0 + pre_act * (1.0 - logistic)))).astype(jnp.bfloat16)
    grad_normed = lax.dot_general(
        grad_pre, hidden_weight, (((1,), (1,)), ((), ())), preferred_element_type=jnp.float32
    )
    grad_cell = inverse * (
        grad_normed
        - jnp.mean(grad_normed, axis=1, keepdims=True)
        - normal_form * jnp.mean(grad_normed * normal_form, axis=1, keepdims=True)
    )
    matrix = stencil_matrix(stencil, weights, lax.axis_size("shard") * mesh_local.shape[0])
    mesh_grad = lax.psum_scatter(
        lax.dot_general(
            matrix,
            grad_cell,
            (((0,), (0,)), ((), ())),
            precision=lax.Precision.HIGHEST,
            preferred_element_type=jnp.float32,
        ).astype(jnp.bfloat16),
        "shard",
        scatter_dimension=0,
        tiled=True,
    ).astype(jnp.float32)
    return mesh_grad[None]


def solution(mesh):
    in_specs = (
        P("member", "shard", None),
        P("shard", None, None),
        P("shard", None, None),
        P("shard", None, None),
        P("shard", None, "member"),
        P("shard", "member"),
        P(),
        P(),
        P(),
        P(),
        P(),
    )
    out_specs = P("member", "shard", None)
    return jax.shard_map(local, mesh=mesh, in_specs=in_specs, out_specs=out_specs, check_vma=False)
```

profile of v0, /device:TPU:2, one launch (start us, length us, event | category | flops | bytes accessed | tf_op | source)
XLA Modules:
  0.0 147.1 jit_solution(18232021255405809372)
XLA Ops:
  6.5 0.9 copy.50
  8.1 18.1 %all-gather = bf16[1,128,1024]{2,1,0:T(8,128)(2,1)S(1)} all-gather(bf16[1,32,1024]{2,1,0:T(8,128)(2,1)} %param.13), channel_id=2, replica_groups=mesh['member'=64,'shard'=4] {'shard'}, dimensions={1}, use_global_device_ids=true | all-gather | bytes 327680 | tf_op jit(solution)/shard_map/all_gather | solution.py:59
  27.7 1.5 %fusion.31 = (f32[768]{0:T(1024)S(1)}, f32[768,1024]{1,0:T(8,128)S(1)}) fusion(f32[768,128]{1,0:T(8,128)S(1)} %select_reduce_fusion, bf16[1,128,1024]{2,1,0:T(8,128)(2,1)S(1)} %all-gather), kind=kOutput, calls=%fused_computation.52 | convolution fusion | flops 1208745216 | bytes 3804160 | tf_op jit(solution)/shard_map/dot_general | solution.py:61
  29.8 1.9 %fusion.9 = f32[768,1024]{1,0:T(8,128)S(1)} fusion(bf16[1024,1024]{1,0:T(8,128)(2,1)S(1)} %copy-done, f32[768,1024]{1,0:T(8,128)S(1)} %get-tuple-element.55, f32[768]{0:T(1024)S(1)} %add_rsqrt_fusion, f32[768]{0:T(1024)S(1)} %broadcast_multiply_fusion.4), kind=kOutput, calls=%fused_computation.19 | convolution fusion | flops 1612972032 | bytes 8394752 | tf_op jit(solution)/shard_map/dot_general | solution.py:29
  31.7 1.7 %copy-done.14 = f32[768,1024]{1,0:T(8,128)} copy-done((f32[768,1024]{1,0:T(8,128)}, f32[768,1024]{1,0:T(8,128)S(1)}, u32[]{:S(2)}) %copy-start.14) | copy-done | bytes 3145752
  33.4 1.1 fusion.25
  34.5 1.0 copy.34
  35.5 8.5 %all-to-all-start = ((f32[1,112,768]{1,0,2:T(1,128)}), f32[1,112,768]{1,0,2:T(1,128)S(1)}, u32[]{:S(2)}, u32[]{:S(2)}) async-start(f32[1,112,768]{1,0,2:T(1,128)} %copy.34), calls=%async_computation | async-start | bytes 786432 | tf_op jit(solution)/shard_map/all_to_all | solution.py:80
  44.8 8.8 %all-to-all-done = f32[1,112,768]{1,0,2:T(1,128)S(1)} async-done(((f32[1,112,768]{1,0,2:T(1,128)}), f32[1,112,768]{1,0,2:T(1,128)S(1)}, u32[]{:S(2)}, u32[]{:S(2)}) %all-to-all-start) | async-done | bytes 344096 | tf_op jit(solution)/shard_map/all_to_all | solution.py:80
  53.6 3.3 %copy.36 = f32[64,1,112,12]{3,2,0,1:T(8,128)} copy(f32[64,1,112,12]{2,1,3,0:T(1,128)S(1)} %bitcast.64) | data formatting | bytes 688128 | tf_op jit(solution)/shard_map/all_to_all | solution.py:80
  56.9 1.3 copy.40
  58.2 3.8 %reshape_reshape.3 = f32[8,8,1344]{2,1,0:T(8,128)} reshape(f32[64,1,112,12]{3,2,0,1:T(8,128)} %copy.36) | data formatting | bytes 688128 | tf_op jit(solution)/shard_map/reshape;reshape | solution.py:86
  62.0 1.2 sub.126
  63.2 18.5 %while.11 = (s32[]{:T(128)}, f32[8,8,1344]{2,1,0:T(8,128)}, f32[8,8,1344]{2,1,0:T(8,128)}, f32[64,112,12]{0,2,1:T(8,128)}, f32[64,1344]{0,1:T(8,128)S(1)}, /*index=5*/s32[]{:T(128)}) while((s32[]{:T(128)}, f32[8,8,1344]{2,1,0:T(8,128)}, f32[8,8,1344]{2,1,0:T(8,128)}, f32[64,112,12]{0,2,1:T(8,128)}, f32[64,1344]{0,1:T(8,128)S(1)}, ...), condition=%wide.wide.region_5.6_spmd, body=%wide.wide.region_3.5_spmd.sunk | while | flops 3429890 | bytes 1292373 | solution.py:91
  63.5 0.8 dynamic-slice_bitcast_fusion.3
  65.8 0.8 dynamic-slice_bitcast_fusion.3
  81.7 1.0 broadcast_multiply_fusion
  82.8 3.9 %mul.93 = f32[64,112,12]{2,1,0:T(8,128)} reshape(f32[8,8,1344]{2,1,0:T(8,128)S(1)} %broadcast_multiply_fusion) | data formatting | bytes 688128 | tf_op jit(solution)/shard_map/mul | solution.py:97
  86.7 2.7 %copy.38 = f32[64,112,12]{1,0,2:T(8,128)S(1)} copy(f32[64,112,12]{2,1,0:T(8,128)} %mul.93) | data formatting | bytes 688128 | tf_op jit(solution)/shard_map/mul | solution.py:97
  89.7 13.7 %all_to_all.33 = bf16[64,112,12]{1,2,0:T(8,128)(2,1)S(1)} all-to-all(bf16[64,112,12]{1,2,0:T(8,128)(2,1)S(1)} %copy.39), channel_id=1, replica_groups=mesh['member'=64,'shard'=4] {'member'}, dimensions={0} | all-to-all | bytes 344064 | tf_op jit(solution)/shard_map/all_to_all | solution.py:100
  103.5 6.1 %fusion.30 = (f32[768]{0:T(1024)S(1)}, f32[768]{0:T(1024)S(1)}, f32[768,1024]{1,0:T(8,128)}) fusion(f32[768]{0:T(1024)S(1)} %add_rsqrt_fusion, f32[768,1024]{1,0:T(8,128)} %copy-done.1, f32[768]{0:T(1024)S(1)} %broadcast_multiply_fusion.4, bf16[1024,1024]{1,0:T(8,128)(2,1)S(1)} %copy-done, f32[768,1024]{1,0:T(8,128)} %copy-done.14, ...), kind=kOutput, calls=%fused_computation.51 | convolution fusion | flops 1798568448 | bytes 11952128 | tf_op jit(solution)/shard_map/dot_general | solution.py:109
  109.7 6.2 %fusion.19 = bf16[128,1024]{1,0:T(8,128)(2,1)} fusion(f32[768,128]{1,0:T(8,128)S(1)} %copy-done.3, f32[768,1024]{1,0:T(8,128)} %get-tuple-element.56, f32[768,1024]{1,0:T(8,128)} %copy-done.1, f32[768]{0:T(1024)S(1)} %get-tuple-element.57, f32[768]{0:T(1024)S(1)} %get-tuple-element.58, f32[768]{0:T(1024)S(1)} %add_rsqrt_fusion, ...), kind=kOutput, calls=%fused_computation.28 | convolution fusion | flops 1212809216 | bytes 6959104 | tf_op jit(solution)/shard_map/dot_general | solution.py:119
  115.9 22.9 %reduce-scatter.2.cloned.1.call-done = bf16[32,1024]{1,0:T(8,128)(2,1)} async-done(((bf16[128,1024]{1,0:T(8,128)(2,1)}), bf16[32,1024]{1,0:T(8,128)(2,1)}) %reduce-scatter.2.cloned.1.call-update) | async-done | bytes 65552 | tf_op jit(solution)/shard_map/reduce_scatter | solution.py:118
  138.8 1.5 %bitcast_convert_fusion = f32[1,32,1024]{2,1,0:T(8,128)} fusion(bf16[32,1024]{1,0:T(8,128)(2,1)} %reduce-scatter.2.cloned.1.call-done), kind=kLoop, calls=%fused_computation.40 | loop fusion | flops 32768 | bytes 196608 | tf_op jit(solution)/shard_map/broadcast_in_dim | solution.py:130
  (73 shorter events, 20.7 us)
Async XLA Ops:
  6.5 23.2 %copy-start = (bf16[1024,1024]{1,0:T(8,128)(2,1)S(1)}, bf16[1024,1024]{1,0:T(8,128)(2,1)}, u32[]{:S(2)}) copy-start(bf16[1024,1024]{1,0:T(8,128)(2,1)} %param.20) | copy-start | bytes 6291460
  27.0 0.8 copy-start.2
  29.2 2.4 %copy-start.1 = (f32[768,1024]{1,0:T(8,128)}, f32[768,1024]{1,0:T(8,128)S(1)}, u32[]{:S(2)}) copy-start(f32[768,1024]{1,0:T(8,128)S(1)} %get-tuple-element.55) | copy-start | bytes 9437188
  29.7 3.7 %copy-start.8 = (f32[1,112,768]{2,1,0:T(8,128)S(1)}, f32[1,112,768]{2,1,0:T(8,128)}, u32[]{:S(2)}) copy-start(f32[1,112,768]{2,1,0:T(8,128)} %param.16) | copy-start | bytes 1032196
  29.7 3.7 %copy-start.9 = (bf16[1024,112]{0,1:T(8,128)(2,1)S(1)}, bf16[1024,112]{0,1:T(8,128)(2,1)}, u32[]{:S(2)}) copy-start(bf16[1024,112]{0,1:T(8,128)(2,1)} %param.22) | copy-start | bytes 688132
  29.7 3.7 %copy-start.11 = (f32[1024]{0:T(1024)S(1)}, f32[1024]{0:T(1024)}, u32[]{:S(2)}) copy-start(f32[1024]{0:T(1024)} %param.21) | copy-start | bytes 12292
  29.8 3.6 %copy-start.13 = (f32[112]{0:T(128)S(1)}, f32[112]{0:T(128)}, u32[]{:S(2)}) copy-start(f32[112]{0:T(128)} %param.23) | copy-start | bytes 1348
  31.7 1.7 %copy-start.14 = (f32[768,1024]{1,0:T(8,128)}, f32[768,1024]{1,0:T(8,128)S(1)}, u32[]{:S(2)}) copy-start(f32[768,1024]{1,0:T(8,128)S(1)} %fusion.9) | copy-start | bytes 9437188
  33.4 10.7 %copy-start.5 = (f32[1,112,12]{1,0,2:T(1,128)S(1)}, f32[1,112,12]{1,0,2:T(1,128)}, u32[]{:S(2)}) copy-start(f32[1,112,12]{1,0,2:T(1,128)} %param.17) | copy-start | bytes 16132
  33.4 10.7 %copy-start.6 = (f32[112]{0:T(128)S(1)}, f32[112]{0:T(128)}, u32[]{:S(2)}) copy-start(f32[112]{0:T(128)} %param.19) | copy-start | bytes 1348
  33.4 10.7 %copy-start.7 = (f32[1,12]{1,0:T(1,128)S(1)}, f32[1,12]{1,0:T(1,128)}, u32[]{:S(2)}) copy-start(f32[1,12]{1,0:T(1,128)} %param.18) | copy-start | bytes 148
  35.5 18.0 %all-to-all-start = ((f32[1,112,768]{1,0,2:T(1,128)}), f32[1,112,768]{1,0,2:T(1,128)S(1)}, u32[]{:S(2)}, u32[]{:S(2)}) async-start(f32[1,112,768]{1,0,2:T(1,128)} %copy.34), calls=%async_computation | async-start | bytes 786432 | tf_op jit(solution)/shard_map/all_to_all | solution.py:80
  44.0 94.7 %reduce-scatter.2.cloned.1.call-start = ((), (), s32[]{:S(2)}) async-start(), calls=%async_computation.3 | async-start | bytes 327680 | tf_op jit(solution)/shard_map/reduce_scatter | solution.py:118
  82.7 6.7 %copy-start.4 = (f32[112,12]{0,1:T(8,128)S(1)}, f32[112,12]{0,1:T(8,128)}, u32[]{:S(2)}) copy-start(f32[112,12]{0,1:T(8,128)} %broadcast_multiply_fusion.1) | copy-start | bytes 16132
  86.7 16.8 %copy-start.10 = (bf16[1024,112]{0,1:T(8,128)(2,1)S(1)}, bf16[1024,112]{0,1:T(8,128)(2,1)}, u32[]{:S(2)}) copy-start(bf16[1024,112]{0,1:T(8,128)(2,1)} %param.22) | copy-start | bytes 688132
  86.7 16.8 %copy-start.12 = (f32[1024]{0:T(1024)S(1)}, f32[1024]{0:T(1024)}, u32[]{:S(2)}) copy-start(f32[1024]{0:T(1024)} %param.21) | copy-start | bytes 12292
  103.5 6.2 %copy-start.3 = (f32[768,128]{1,0:T(8,128)S(1)}, f32[768,128]{1,0:T(8,128)}, u32[]{:S(2)}) copy-start(f32[768,128]{1,0:T(8,128)} %copy-done.2) | copy-start | bytes 1179652
Sparse Core Ops, SparseCore 0:
  116.0 22.7 reduce-scatter.1
where the time goes:
time: 148 us; the launch traced here: 147 us
  local copies, waits for them, and re-layouts  34.9 us (24%)
  blocking collectives  31.8 us (21%)
  waiting for transfers between devices  31.7 us (21%)
  matrix products  16.8 us (11%)
  between operations  13.7 us (9%)
  other arithmetic  9.67 us (7%)
  starting transfers between devices  8.52 us (6%)
    reduce_scatter x1, waiting for transfers between devices, local(): lax.psum_scatter(lax.dot_general(matrix, grad_cell, (((0,), (0,)), ((), (...  22.9 us
    all_gather x1, blocking collectives, local(): shard_rows = lax.all_gather(mesh_local, 'shard', axis=0, tiled=True)  18.1 us
    all_to_all x1, blocking collectives, local(): lax.all_to_all(slopes, 'member', split_axis=0, concat_axis=2, tiled=True)[0]  13.7 us
    sub x17, local copies, waits for them, and re-layouts, group_pairs(): return jnp.sum(softened_slope(chosen[:, None] - flattened[None]), axis=1)  9.59 us
    all_to_all x1, waiting for transfers between devices, local(): lax.all_to_all(prediction_piece[None], 'member', split_axis=2, concat_axi...  8.79 us
    all_to_all x1, starting transfers between devices, local(): lax.all_to_all(prediction_piece[None], 'member', split_axis=2, concat_axi...  8.48 us
    mul x2, local copies, waits for them, and re-layouts, local(): (1.0 - fairness_factor) / (members - 1) * pairwise_sums  6.63 us
    dot_general x1, matrix products, local(): lax.dot_general(matrix, grad_cell, (((0,), (0,)), ((), ())), precision=la...  6.18 us
  transfers between devices with their start and end apart: 2, of which 2 were waited for; matrix products, arithmetic and copies ran while one was open for 0% of the time, Pallas kernels for 0%

commit v1 on v0

--- a/solution.py
+++ b/solution.py
@@ -56,7 +56,15 @@
     variables = previous.shape[0]
     members = lax.axis_size("member")
     block_cells = cell_count // members
-    shard_rows = lax.all_gather(mesh_local, "shard", axis=0, tiled=True)
+    shard_rows = jnp.concatenate(
+        lax.all_to_all(
+            jnp.stack([mesh_local] * lax.psum(1, axis_name="shard")),
+            axis_name="shard",
+            split_axis=0,
+            concat_axis=0,
+        ),
+        axis=0,
+    )
     matrix = stencil_matrix(stencil, weights, shard_rows.shape[0])
     latent = jnp.dot(
         matrix,

time: 148 us -> 146 us (0.986)
  blocking collectives: 31.8 us -> 13.7 us
  starting transfers between devices: 8.52 us -> 16.7 us
  waiting for transfers between devices: 31.7 us -> 38.5 us
    all_gather x1 -> x0, blocking collectives: 18.1 us -> none  [local(): shard_rows = lax.all_gather(mesh_local, 'shard', axis=0, tiled=True)]
    all_to_all x0 -> x1, waiting for transfers between devices: none -> 8.53 us  [local(): lax.all_to_all(jnp.stack([mesh_local] * lax.psum(1, axis_name='shard')),...]
    all_to_all x0 -> x1, starting transfers between devices: none -> 8.46 us  [local(): lax.all_to_all(jnp.stack([mesh_local] * lax.psum(1, axis_name='shard')),...]
    another operation x0 -> x1, local copies, waits for them, and re-layouts: none -> 1.71 us  [local(): jnp.stack([mesh_local] * lax.psum(1, axis_name='shard'))]
    reduce_scatter x1, waiting for transfers between devices: 22.9 us -> 21.2 us  [local(): lax.psum_scatter(lax.dot_general(matrix, grad_cell, (((0,), (0,)), ((), (...]
  transfers between devices with their start and end apart: 2 -> 3, of which waited for: 2 -> 3; matrix products, arithmetic and copies ran while one was open for 0% -> 2% of each run, Pallas kernels for 0% -> 0%
where the time goes in v1:
time: 146 us; the launch traced here: 145 us
  waiting for transfers between devices  38.5 us (26%)
  local copies, waits for them, and re-layouts  35.8 us (25%)
  starting transfers between devices  16.7 us (11%)
  matrix products  16.7 us (11%)
  blocking collectives  13.7 us (9%)
  between operations  13.7 us (9%)
  other arithmetic  9.67 us (7%)
    reduce_scatter x1, waiting for transfers between devices, local(): lax.psum_scatter(lax.dot_general(matrix, grad_cell, (((0,), (0,)), ((), (...  21.2 us
    all_to_all x1, blocking collectives, local(): lax.all_to_all(slopes, 'member', split_axis=0, concat_axis=2, tiled=True)[0]  13.7 us
    sub x17, local copies, waits for them, and re-layouts, group_pairs(): return jnp.sum(softened_slope(chosen[:, None] - flattened[None]), axis=1)  9.59 us
    all_to_all x1, waiting for transfers between devices, local(): lax.all_to_all(prediction_piece[None], 'member', split_axis=2, concat_axi...  8.79 us
    all_to_all x1, waiting for transfers between devices, local(): lax.all_to_all(jnp.stack([mesh_local] * lax.psum(1, axis_name='shard')),...  8.53 us
    all_to_all x1, starting transfers between devices, local(): lax.all_to_all(jnp.stack([mesh_local] * lax.psum(1, axis_name='shard')),...  8.46 us
    all_to_all x1, starting transfers between devices, local(): lax.all_to_all(prediction_piece[None], 'member', split_axis=2, concat_axi...  8.24 us
    mul x2, local copies, waits for them, and re-layouts, local(): (1.0 - fairness_factor) / (members - 1) * pairwise_sums  6.64 us
  transfers between devices with their start and end apart: 3, of which 3 were waited for; matrix products, arithmetic and copies ran while one was open for 2% of the time, Pallas kernels for 0%

profile of v1, /device:TPU:2, one launch (start us, length us, event | category | flops | bytes accessed | tf_op | source)
XLA Modules:
  0.0 144.9 jit_solution(5145250977044270354)
XLA Ops:
  6.5 1.7 %stack.3 = bf16[4,32,1024]{2,1,0:T(8,128)(2,1)} broadcast(bf16[32,1024]{1,0:T(8,128)(2,1)} %bitcast.69), dimensions={1,2} | broadcast | bytes 327680 | tf_op jit(solution)/shard_map/stack | solution.py:61
  8.2 8.5 %all-to-all-start = ((bf16[4,32,1024]{2,1,0:T(8,128)(2,1)}), bf16[4,32,1024]{2,1,0:T(8,128)(2,1)S(1)}, u32[]{:S(2)}, u32[]{:S(2)}) async-start(bf16[4,32,1024]{2,1,0:T(8,128)(2,1)} %stack.3), calls=%async_computation | async-start | bytes 524288 | tf_op jit(solution)/shard_map/all_to_all | solution.py:60
  18.9 8.5 %all-to-all-done = bf16[4,32,1024]{2,1,0:T(8,128)(2,1)S(1)} async-done(((bf16[4,32,1024]{2,1,0:T(8,128)(2,1)}), bf16[4,32,1024]{2,1,0:T(8,128)(2,1)S(1)}, u32[]{:S(2)}, u32[]{:S(2)}) %all-to-all-start) | async-done | bytes 262176 | tf_op jit(solution)/shard_map/all_to_all | solution.py:60
  27.4 1.5 %fusion.29 = (f32[768]{0:T(1024)S(1)}, f32[768,1024]{1,0:T(8,128)S(1)}) fusion(f32[768,128]{1,0:T(8,128)S(1)} %select_reduce_fusion, bf16[128,1024]{1,0:T(8,128)(2,1)S(1)} %bitcast.67), kind=kOutput, calls=%fused_computation.50 | convolution fusion | flops 1208745216 | bytes 3804160 | tf_op jit(solution)/shard_map/dot_general | solution.py:69
  29.5 1.9 %fusion.9 = f32[768,1024]{1,0:T(8,128)S(1)} fusion(bf16[1024,1024]{1,0:T(8,128)(2,1)S(1)} %copy-done, f32[768,1024]{1,0:T(8,128)S(1)} %get-tuple-element.55, f32[768]{0:T(1024)S(1)} %add_rsqrt_fusion, f32[768]{0:T(1024)S(1)} %broadcast_multiply_fusion.4), kind=kOutput, calls=%fused_computation.19 | convolution fusion | flops 1612972032 | bytes 8394752 | tf_op jit(solution)/shard_map/dot_general | solution.py:29
  31.4 1.7 %copy-done.14 = f32[768,1024]{1,0:T(8,128)} copy-done((f32[768,1024]{1,0:T(8,128)}, f32[768,1024]{1,0:T(8,128)S(1)}, u32[]{:S(2)}) %copy-start.14) | copy-done | bytes 3145752
  33.1 1.1 fusion.25
  34.2 1.0 copy.34
  35.2 8.2 %all-to-all-start.1 = ((f32[1,112,768]{1,0,2:T(1,128)}), f32[1,112,768]{1,0,2:T(1,128)S(1)}, u32[]{:S(2)}, u32[]{:S(2)}) async-start(f32[1,112,768]{1,0,2:T(1,128)} %copy.34), calls=%async_computation.1 | async-start | bytes 786432 | tf_op jit(solution)/shard_map/all_to_all | solution.py:88
  44.2 8.8 %all-to-all-done.1 = f32[1,112,768]{1,0,2:T(1,128)S(1)} async-done(((f32[1,112,768]{1,0,2:T(1,128)}), f32[1,112,768]{1,0,2:T(1,128)S(1)}, u32[]{:S(2)}, u32[]{:S(2)}) %all-to-all-start.1) | async-done | bytes 344096 | tf_op jit(solution)/shard_map/all_to_all | solution.py:88
  53.0 3.3 %copy.36 = f32[64,1,112,12]{3,2,0,1:T(8,128)} copy(f32[64,1,112,12]{2,1,3,0:T(1,128)S(1)} %bitcast.62) | data formatting | bytes 688128 | tf_op jit(solution)/shard_map/all_to_all | solution.py:88
  56.3 1.3 copy.40
  57.6 3.8 %reshape_reshape.3 = f32[8,8,1344]{2,1,0:T(8,128)} reshape(f32[64,1,112,12]{3,2,0,1:T(8,128)} %copy.36) | data formatting | bytes 688128 | tf_op jit(solution)/shard_map/reshape;reshape | solution.py:94
  61.5 1.2 sub.126
  62.7 18.5 %while.11 = (s32[]{:T(128)}, f32[8,8,1344]{2,1,0:T(8,128)}, f32[8,8,1344]{2,1,0:T(8,128)}, f32[64,112,12]{0,2,1:T(8,128)}, f32[64,1344]{0,1:T(8,128)S(1)}, /*index=5*/s32[]{:T(128)}) while((s32[]{:T(128)}, f32[8,8,1344]{2,1,0:T(8,128)}, f32[8,8,1344]{2,1,0:T(8,128)}, f32[64,112,12]{0,2,1:T(8,128)}, f32[64,1344]{0,1:T(8,128)S(1)}, ...), condition=%wide.wide.region_5.6_spmd, body=%wide.wide.region_3.5_spmd.sunk | while | flops 3429890 | bytes 1292373 | solution.py:99
  65.3 0.8 dynamic-slice_bitcast_fusion.3
  81.2 1.0 broadcast_multiply_fusion
  82.2 3.9 %mul.93 = f32[64,112,12]{2,1,0:T(8,128)} reshape(f32[8,8,1344]{2,1,0:T(8,128)S(1)} %broadcast_multiply_fusion) | data formatting | bytes 688128 | tf_op jit(solution)/shard_map/mul | solution.py:105
  86.2 2.7 %copy.38 = f32[64,112,12]{1,0,2:T(8,128)S(1)} copy(f32[64,112,12]{2,1,0:T(8,128)} %mul.93) | data formatting | bytes 688128 | tf_op jit(solution)/shard_map/mul | solution.py:105
  89.2 13.7 %all_to_all.38 = bf16[64,112,12]{1,2,0:T(8,128)(2,1)S(1)} all-to-all(bf16[64,112,12]{1,2,0:T(8,128)(2,1)S(1)} %copy.39), channel_id=1, replica_groups=mesh['member'=64,'shard'=4] {'member'}, dimensions={0} | all-to-all | bytes 344064 | tf_op jit(solution)/shard_map/all_to_all | solution.py:108
  103.0 6.1 %fusion.28 = (f32[768]{0:T(1024)S(1)}, f32[768]{0:T(1024)S(1)}, f32[768,1024]{1,0:T(8,128)}) fusion(f32[768]{0:T(1024)S(1)} %add_rsqrt_fusion, f32[768,1024]{1,0:T(8,128)} %copy-done.1, f32[768]{0:T(1024)S(1)} %broadcast_multiply_fusion.4, bf16[1024,1024]{1,0:T(8,128)(2,1)S(1)} %copy-done, f32[768,1024]{1,0:T(8,128)} %copy-done.14, ...), kind=kOutput, calls=%fused_computation.49 | convolution fusion | flops 1798568448 | bytes 11952128 | tf_op jit(solution)/shard_map/dot_general | solution.py:117
  109.1 6.2 %fusion.19 = bf16[128,1024]{1,0:T(8,128)(2,1)} fusion(f32[768,128]{1,0:T(8,128)S(1)} %copy-done.3, f32[768,1024]{1,0:T(8,128)} %get-tuple-element.56, f32[768,1024]{1,0:T(8,128)} %copy-done.1, f32[768]{0:T(1024)S(1)} %get-tuple-element.57, f32[768]{0:T(1024)S(1)} %get-tuple-element.58, f32[768]{0:T(1024)S(1)} %add_rsqrt_fusion, ...), kind=kOutput, calls=%fused_computation.28 | convolution fusion | flops 1212809216 | bytes 6959104 | tf_op jit(solution)/shard_map/dot_general | solution.py:127
  115.4 21.2 %reduce-scatter.2.cloned.1.call-done = bf16[32,1024]{1,0:T(8,128)(2,1)} async-done(((bf16[128,1024]{1,0:T(8,128)(2,1)}), bf16[32,1024]{1,0:T(8,128)(2,1)}) %reduce-scatter.2.cloned.1.call-update) | async-done | bytes 65552 | tf_op jit(solution)/shard_map/reduce_scatter | solution.py:126
  136.6 1.5 %bitcast_convert_fusion = f32[1,32,1024]{2,1,0:T(8,128)} fusion(bf16[32,1024]{1,0:T(8,128)(2,1)} %reduce-scatter.2.cloned.1.call-done), kind=kLoop, calls=%fused_computation.38 | loop fusion | flops 32768 | bytes 196608 | tf_op jit(solution)/shard_map/broadcast_in_dim | solution.py:138
  (75 shorter events, 21.4 us)
Async XLA Ops:
  6.5 22.9 %copy-start = (bf16[1024,1024]{1,0:T(8,128)(2,1)S(1)}, bf16[1024,1024]{1,0:T(8,128)(2,1)}, u32[]{:S(2)}) copy-start(bf16[1024,1024]{1,0:T(8,128)(2,1)} %param.20) | copy-start | bytes 6291460
  8.2 19.2 %all-to-all-start = ((bf16[4,32,1024]{2,1,0:T(8,128)(2,1)}), bf16[4,32,1024]{2,1,0:T(8,128)(2,1)S(1)}, u32[]{:S(2)}, u32[]{:S(2)}) async-start(bf16[4,32,1024]{2,1,0:T(8,128)(2,1)} %stack.3), calls=%async_computation | async-start | bytes 524288 | tf_op jit(solution)/shard_map/all_to_all | solution.py:60
  18.9 10.5 %copy-start.2 = (f32[768,128]{1,0:T(8,128)}, f32[768,128]{1,0:T(8,128)S(1)}, u32[]{:S(2)}) copy-start(f32[768,128]{1,0:T(8,128)S(1)} %select_reduce_fusion) | copy-start | bytes 1179652
  28.9 2.4 %copy-start.1 = (f32[768,1024]{1,0:T(8,128)}, f32[768,1024]{1,0:T(8,128)S(1)}, u32[]{:S(2)}) copy-start(f32[768,1024]{1,0:T(8,128)S(1)} %get-tuple-element.55) | copy-start | bytes 9437188
  29.4 3.7 %copy-start.8 = (f32[1,112,768]{2,1,0:T(8,128)S(1)}, f32[1,112,768]{2,1,0:T(8,128)}, u32[]{:S(2)}) copy-start(f32[1,112,768]{2,1,0:T(8,128)} %param.16) | copy-start | bytes 1032196
  29.4 3.7 %copy-start.9 = (bf16[1024,112]{0,1:T(8,128)(2,1)S(1)}, bf16[1024,112]{0,1:T(8,128)(2,1)}, u32[]{:S(2)}) copy-start(bf16[1024,112]{0,1:T(8,128)(2,1)} %param.22) | copy-start | bytes 688132
  29.4 3.6 %copy-start.11 = (f32[1024]{0:T(1024)S(1)}, f32[1024]{0:T(1024)}, u32[]{:S(2)}) copy-start(f32[1024]{0:T(1024)} %param.21) | copy-start | bytes 12292
  29.5 3.6 %copy-start.13 = (f32[112]{0:T(128)S(1)}, f32[112]{0:T(128)}, u32[]{:S(2)}) copy-start(f32[112]{0:T(128)} %param.23) | copy-start | bytes 1348
  31.4 1.7 %copy-start.14 = (f32[768,1024]{1,0:T(8,128)}, f32[768,1024]{1,0:T(8,128)S(1)}, u32[]{:S(2)}) copy-start(f32[768,1024]{1,0:T(8,128)S(1)} %fusion.9) | copy-start | bytes 9437188
  33.1 10.4 %copy-start.5 = (f32[1,112,12]{1,0,2:T(1,128)S(1)}, f32[1,112,12]{1,0,2:T(1,128)}, u32[]{:S(2)}) copy-start(f32[1,112,12]{1,0,2:T(1,128)} %param.17) | copy-start | bytes 16132
  33.1 10.4 %copy-start.6 = (f32[112]{0:T(128)S(1)}, f32[112]{0:T(128)}, u32[]{:S(2)}) copy-start(f32[112]{0:T(128)} %param.19) | copy-start | bytes 1348
  33.1 10.4 %copy-start.7 = (f32[1,12]{1,0:T(1,128)S(1)}, f32[1,12]{1,0:T(1,128)}, u32[]{:S(2)}) copy-start(f32[1,12]{1,0:T(1,128)} %param.18) | copy-start | bytes 148
  35.2 17.8 %all-to-all-start.1 = ((f32[1,112,768]{1,0,2:T(1,128)}), f32[1,112,768]{1,0,2:T(1,128)S(1)}, u32[]{:S(2)}, u32[]{:S(2)}) async-start(f32[1,112,768]{1,0,2:T(1,128)} %copy.34), calls=%async_computation.1 | async-start | bytes 786432 | tf_op jit(solution)/shard_map/all_to_all | solution.py:88
  43.5 93.1 %reduce-scatter.2.cloned.1.call-start = ((), (), s32[]{:S(2)}) async-start(), calls=%async_computation.4 | async-start | bytes 327680 | tf_op jit(solution)/shard_map/reduce_scatter | solution.py:126
  82.2 6.7 %copy-start.4 = (f32[112,12]{0,1:T(8,128)S(1)}, f32[112,12]{0,1:T(8,128)}, u32[]{:S(2)}) copy-start(f32[112,12]{0,1:T(8,128)} %broadcast_multiply_fusion.1) | copy-start | bytes 16132
  86.2 16.8 %copy-start.10 = (bf16[1024,112]{0,1:T(8,128)(2,1)S(1)}, bf16[1024,112]{0,1:T(8,128)(2,1)}, u32[]{:S(2)}) copy-start(bf16[1024,112]{0,1:T(8,128)(2,1)} %param.22) | copy-start | bytes 688132
  86.2 16.8 %copy-start.12 = (f32[1024]{0:T(1024)S(1)}, f32[1024]{0:T(1024)}, u32[]{:S(2)}) copy-start(f32[1024]{0:T(1024)} %param.21) | copy-start | bytes 12292
  103.0 6.1 %copy-start.3 = (f32[768,128]{1,0:T(8,128)S(1)}, f32[768,128]{1,0:T(8,128)}, u32[]{:S(2)}) copy-start(f32[768,128]{1,0:T(8,128)} %copy-done.2) | copy-start | bytes 1179652
Sparse Core Ops, SparseCore 0:
  115.5 21.0 reduce-scatter.1
